TPU v7x, 128 devices: a whole 4x4x4 slice. The times are simulated.
128 devices in a mesh: replica: 8 (over z_hi, y), tensor: 16 (over x, z_lo, core).
Axes of the slice: x: 4, y: 4, z: 4 (z_hi: 2, z_lo: 2; z = z_hi * 2 + z_lo), core: 2. Of those that a mesh axis runs over, the one named last changes fastest.
Arguments:
- queries: bfloat16 [1024, 8192], P('replica', 'tensor'), may hold values from -200 to 200
- new_kv: bfloat16 [1024, 1024], P('replica'), may hold values from -8 to 8
- kv_pool: bfloat16 [1024, 64, 1024], P(('replica', 'tensor')), may hold values from -6 to 6
- anchor: int32 [8, 8], replicated, may hold values from 0 to 7, as said below
- page_table: int32 [64, 16], replicated, may hold values from 0 to 7, as said below
- prefix_len: int32 [64], replicated, may hold values from 1 to 1024, 32768 in all
- turn_rows: int32 [8, 8], replicated, may hold values from 1 to 32, 128 in all within a row
- out_weight: bfloat16 [8192, 16384], P('tensor', 'replica'), may hold values from -0.5 to 0.5
- residual: bfloat16 [1024, 16384], P(None, 'replica'), may hold values from -400 to 400
- norm_gain: bfloat16 [16384], P('replica'), may hold values from 0.099609375 to 1.8984375
- gate_up: bfloat16 [16384, 2, 26624], P('replica', None, 'tensor'), may hold values from -0.046875 to 0.046875
Outputs:
- hidden: bfloat16 [1024, 26624], P('replica', 'tensor')
Inputs may be any that keep to these rules, and one draw needn't show every extreme that they name: Slot j of new replica d holds session anchor[d, j] of old replica j; for each old replica, the 8 slots that come from it name each of its 8 sessions exactly once. `page_table`: row o * 8 + s lists the pages of session s of old replica o: entry k is a local page index on device k of that replica's 16 tensor devices, whose pages are numbered (o * 16 + k) * 8 + index in kv_pool; on each device the 8 sessions use distinct pages. `prefix_len`: indexed by d * 8 + j for slot j of new replica d. `turn_rows`: each replica's entries sum to 128.
All inputs are finite; a program needn't handle non-finite values.
Results may differ from a plain program's by a relative error of at most 0.0064.
Values may be sent and summed in bfloat16 or wider, within the bound.
A program may use at most 128 MiB of HBM per device.

v0:
```python
import jax
import jax.numpy as jnp
import numpy as np
from jax import lax
from jax.sharding import PartitionSpec as P

D = 16384
HD = 128
HEADS = 64
KVH = 4
PAGE = 64
SHARE = 1
ROWS = 128
GROUP = 16
EPSILON = 1e-05


def per_device(
    queries,
    new_kv,
    kv_pool,
    anchor,
    page_table,
    prefix_len,
    turn_rows,
    out_weight,
    residual,
    norm_gain,
    gate_up,
):
    replicas = lax.axis_size("replica")
    tensors = lax.axis_size("tensor")
    replica_idx = lax.axis_index("replica")
    tensor_idx = lax.axis_index("tensor")
    sessions = SHARE * replicas
    heads_local = HEADS // tensors
    pair_width = 2 * HD
    cached_len = tensors * PAGE
    owner_head = np.arange(tensors) * heads_local // GROUP
    from_here = lax.dynamic_slice_in_dim(anchor, replica_idx * SHARE, SHARE, 1)
    table_rows = lax.dynamic_slice_in_dim(page_table, replica_idx * sessions, sessions, 0)
    my_column = lax.dynamic_slice_in_dim(table_rows, tensor_idx, 1, 1)[:, 0]
    page_index = jnp.take(my_column, from_here.reshape(-1), axis=0)
    chosen = jnp.take(kv_pool, page_index, axis=0).reshape(replicas, SHARE, PAGE, KVH, pair_width)
    outgoing = jnp.take(chosen, owner_head, axis=3)
    outgoing = jnp.transpose(outgoing, (0, 3, 1, 2, 4)).reshape(
        replicas * tensors, SHARE, PAGE, pair_width
    )
    arrived = lax.all_to_all(
        outgoing, ("replica", "tensor"), split_axis=0, concat_axis=0, tiled=True
    )
    arrived = arrived.reshape(replicas, tensors, SHARE, PAGE, pair_width)
    prefix_blocks = jnp.transpose(arrived, (0, 2, 1, 3, 4)).reshape(
        sessions, cached_len, pair_width
    )
    kv_group = tensor_idx * heads_local // GROUP
    fresh_pair = lax.dynamic_slice_in_dim(new_kv, kv_group * pair_width, pair_width, 1)
    rows_here = queries.shape[0]
    slot_rows = ROWS // 4
    query_heads = queries.reshape(rows_here, heads_local, HD)
    counts = lax.dynamic_slice_in_dim(turn_rows, replica_idx, 1, 0)[0]
    bounds = jnp.cumsum(counts, dtype=jnp.int32)
    starts = bounds - counts
    row_ids = jnp.arange(rows_here, dtype=jnp.int32)
    row_slot = jnp.sum(
        (row_ids[:, None] >= bounds[None, :]).astype(jnp.int32), axis=1, dtype=jnp.int32
    )
    offsets = jnp.arange(slot_rows, dtype=jnp.int32)
    padded_index = jnp.minimum(starts[:, None] + offsets[None, :], rows_here - 1).reshape(-1)
    slot_queries = jnp.take(query_heads, padded_index, axis=0).reshape(
        sessions, slot_rows, heads_local, HD
    )
    slot_fresh = jnp.take(fresh_pair, padded_index, axis=0).reshape(sessions, slot_rows, pair_width)
    lengths = lax.dynamic_slice_in_dim(prefix_len, replica_idx * sessions, sessions, 0)
    key_pos = jnp.arange(cached_len, dtype=jnp.int32)
    prefix_mask = (key_pos[None, :] < lengths[:, None])[:, None, :]
    fresh_mask = (offsets[None, None, :] <= offsets[None, :, None]) & (
        offsets[None, None, :] < counts[:, None, None]
    )
    score_scale = HD ** (-0.5)
    prefix_scores = (
        jnp.einsum(
            "smhd,skd->hsmk",
            slot_queries,
            prefix_blocks[:, :, :HD],
            preferred_element_type=jnp.float32,
        )
        * score_scale
    )
    fresh_scores = (
        jnp.einsum(
            "smhd,snd->hsmn",
            slot_queries,
            slot_fresh[:, :, :HD],
            preferred_element_type=jnp.float32,
        )
        * score_scale
    )
    prefix_scores = jnp.where(prefix_mask[None], prefix_scores, -jnp.inf)
    fresh_scores = jnp.where(fresh_mask[None], fresh_scores, -jnp.inf)
    row_peak = jnp.maximum(jnp.max(prefix_scores, axis=3), jnp.max(fresh_scores, axis=3))
    prefix_weights = jnp.exp(prefix_scores - row_peak[..., None])
    fresh_weights = jnp.exp(fresh_scores - row_peak[..., None])
    denominator = jnp.sum(prefix_weights, axis=3) + jnp.sum(fresh_weights, axis=3)
    mixed_values = jnp.einsum(
        "hsmk,skd->smhd",
        prefix_weights.astype(jnp.bfloat16),
        prefix_blocks[:, :, HD:],
        preferred_element_type=jnp.float32,
    )
    mixed_values = mixed_values + jnp.einsum(
        "hsmn,snd->smhd",
        fresh_weights.astype(jnp.bfloat16),
        slot_fresh[:, :, HD:],
        preferred_element_type=jnp.float32,
    )
    slot_attended = (mixed_values / jnp.transpose(denominator, (1, 2, 0))[..., None]).astype(
        jnp.bfloat16
    )
    slot_attended = slot_attended.reshape(sessions * slot_rows, heads_local * HD)
    back_index = row_slot * slot_rows + row_ids - jnp.take(starts, row_slot, axis=0)
    attended = jnp.take(slot_attended, back_index, axis=0)
    partial_out = jnp.dot(
        lax.all_gather(attended, "replica", axis=0, tiled=True),
        out_weight,
        preferred_element_type=jnp.float32,
    )
    weights_local = gate_up.reshape(gate_up.shape[0], 2 * gate_up.shape[2])
    gain_row = norm_gain.astype(jnp.float32)
    carried = residual.astype(jnp.float32) + lax.psum(partial_out, "tensor")
    squares = lax.psum(jnp.sum(carried * carried, axis=1), "replica")
    normed = (carried * lax.rsqrt(squares / D + EPSILON)[:, None] * gain_row[None, :]).astype(
        jnp.bfloat16
    )
    summed = lax.psum_scatter(
        jnp.dot(normed, weights_local, preferred_element_type=jnp.float32),
        "replica",
        scatter_dimension=0,
        tiled=True,
    )
    paired = summed.reshape(rows_here, 2, gate_up.shape[2])
    return (jax.nn.silu(paired[:, 0, :]) * paired[:, 1, :]).astype(jnp.bfloat16)


def solution(mesh):
    placed = (
        P("replica", "tensor"),
        P("replica", None),
        P(("replica", "tensor"), None, None),
        P(),
        P(),
        P(),
        P(),
        P("tensor", "replica"),
        P(None, "replica"),
        P("replica"),
        P("replica", None, "tensor"),
    )
    return jax.shard_map(
        per_device, mesh=mesh, in_specs=placed, out_specs=P("replica", "tensor"), check_vma=False
    )
```

profile of v0, /device:TPU:0, one launch (start us, length us, event | category | flops | bytes accessed | tf_op | source)
XLA Modules:
  0.0 568.3 jit_solution(5678871009920733186)
XLA Ops:
  6.5 0.0 copy-start
  6.5 0.9 constant_dynamic-slice_fusion
  7.4 0.1 copy.62
  7.6 0.8 dynamic-slice_bitcast_fusion
  8.3 0.6 gather_fusion
  9.0 0.7 pad_clamp_fusion.2
  9.7 1.8 gather_fusion.1
  11.5 1.6 gather.42
  13.1 1.4 fusion.18
  14.5 2.8 gather_fusion.2
  17.3 4.7 copy.48
  22.0 0.0 copy-start.4
  22.0 0.0 copy-start.2
  22.0 11.7 %all-to-all-start = ((bf16[128,1,64,256]{3,2,1,0:T(8,128)(2,1)}), bf16[128,1,64,256]{3,2,1,0:T(8,128)(2,1)}, u32[]{:S(2)}, u32[]{:S(2)}) async-start(bf16[128,1,64,256]{3,2,1,0:T(8,128)(2,1)} %bitcast.135), calls=%async_computation | async-start | bytes 8388608 | tf_op jit(solution)/shard_map/all_to_all | solution.py:49
  33.7 0.0 all-gather.2.cloned.1.call-start
  33.8 0.0 copy-done.4
  33.8 0.1 dynamic_slice.19
  33.9 0.7 fusion.33
  34.5 0.2 reduce-window.7
  34.7 0.7 bitcast_subtract_fusion.1
  35.4 0.1 add_minimum_fusion
  35.5 0.1 min.22
  35.6 0.0 copy-done.2
  35.7 0.9 constant_dynamic-slice_fusion.1
  36.5 1.1 gather_fusion.4
  37.7 1.0 gather_fusion.3
  38.7 0.7 fusion.39
  39.4 0.1 convert_reduce_fusion
  39.5 4.9 compare_and_fusion.1
  44.4 0.1 compare_and_fusion
  44.4 0.1 iota_compare_fusion.2
  44.5 0.1 iota_compare_fusion
  44.6 0.1 broadcast_and_fusion
  44.7 0.1 broadcast_select_fusion.2
  44.8 0.6 fusion.40
  45.4 40.4 %all-to-all-done = bf16[128,1,64,256]{3,2,1,0:T(8,128)(2,1)} async-done(((bf16[128,1,64,256]{3,2,1,0:T(8,128)(2,1)}), bf16[128,1,64,256]{3,2,1,0:T(8,128)(2,1)}, u32[]{:S(2)}, u32[]{:S(2)}) %all-to-all-start) | async-done | bytes 4194336 | tf_op jit(solution)/shard_map/all_to_all | solution.py:49
  85.8 2.4 bitcast_reduce_fusion
  88.3 2.7 fusion.6
  91.0 1.0 fusion.4
  92.0 0.1 fusion.21
  92.2 0.3 fusion.17
  92.5 0.1 copy.54
  92.7 0.8 gather_fusion.5
  93.5 0.7 broadcast_select_fusion.1
  94.3 0.0 all-gather.2.cloned.1.call-update
  94.3 0.0 all-reduce.2.cloned.1.call-start
  94.4 47.4 %all-gather.2.cloned.1.call-done = bf16[1024,512]{1,0:T(8,128)(2,1)} async-done(((bf16[128,512]{1,0:T(8,128)(2,1)}), bf16[1024,512]{1,0:T(8,128)(2,1)}) %all-gather.2.cloned.1.call-update) | async-done | bytes 1048592 | tf_op jit(solution)/shard_map/all_gather | solution.py:124
  141.7 0.0 copy-done
  141.7 6.8 %fusion.41 = f32[1024,2048]{1,0:T(8,128)} fusion(bf16[1024,512]{1,0:T(8,128)(2,1)} %all-gather.2.cloned.1.call-done, bf16[512,2048]{1,0:T(8,128)(2,1)S(1)} %copy-done), kind=kOutput, calls=%fused_computation.105 | convolution fusion | flops 2147483648 | bytes 11534336 | tf_op jit(solution)/shard_map/dot_general | solution.py:123
  148.5 0.0 all-reduce.2.cloned.1.call-update
  148.6 0.0 reduce-scatter.2.cloned.1.call-start
  148.6 0.6 copy-done.3
  149.2 14.3 %copy.66 = bf16[256,8,2,1664]{3,1,2,0:T(8,128)(2,1)} copy(bf16[256,8,2,1664]{3,2,1,0:T(2,128)(2,1)} %bitcast.137) | data formatting | bytes 27262976
  163.5 177.2 %all-reduce.2.cloned.1.call-done = f32[1024,2048]{1,0:T(8,128)} async-done(((f32[1024,2048]{1,0:T(8,128)}), f32[1024,2048]{1,0:T(8,128)}) %all-reduce.2.cloned.1.call-update) | async-done | bytes 8388624 | tf_op jit(solution)/shard_map/psum | solution.py:130
  340.7 5.7 %multiply_reduce_fusion = f32[1024]{0:T(1024)S(1)} fusion(f32[1024,2048]{1,0:T(8,128)} %all-reduce.2.cloned.1.call-done, bf16[1024,2048]{1,0:T(8,128)(2,1)} %param.20), kind=kLoop, calls=%fused_computation.7 | loop fusion | flops 8387584 | bytes 12587008 | tf_op jit(solution)/shard_map/reduce_sum | solution.py:131
  346.4 23.9 %psum.15 = f32[1024]{0:T(1024)S(1)} all-reduce(f32[1024]{0:T(1024)S(1)} %multiply_reduce_fusion), channel_id=1, replica_groups=mesh['replica'=8,'tensor'=16] {'replica'}, use_global_device_ids=true, to_apply=%region_8.9 | all-reduce | flops 1024 | bytes 8192 | tf_op jit(solution)/shard_map/psum | solution.py:131
  370.3 24.2 %fusion = f32[1024,3328]{1,0:T(8,128)} fusion(bf16[2048,3328]{1,0:T(8,128)(2,1)} %bitcast.138, f32[1024,2048]{1,0:T(8,128)} %all-reduce.2.cloned.1.call-done, bf16[1024,2048]{1,0:T(8,128)(2,1)} %param.20, f32[2048]{0:T(1024)S(1)} %convert_element_type.29, f32[1024]{0:T(1024)S(1)} %add_rsqrt_fusion), kind=kOutput, calls=%fused_computation.9 | convolution fusion | flops 13969129472 | bytes 39858176 | tf_op jit(solution)/shard_map/dot_general | solution.py:136
  394.5 0.0 reduce-scatter.2.cloned.1.call-update
  394.6 0.0 copy-start.1
  394.6 159.6 %reduce-scatter.2.cloned.1.call-done = f32[128,3328]{1,0:T(8,128)} async-done(((f32[1024,3328]{1,0:T(8,128)}), f32[128,3328]{1,0:T(8,128)}) %reduce-scatter.2.cloned.1.call-update) | async-done | bytes 1703952 | tf_op jit(solution)/shard_map/reduce_scatter | solution.py:135
  554.2 3.1 reshape.267
  557.3 3.4 fusion.38
  560.7 1.0 fusion.20
  561.7 0.0 copy-done.1
  (17 shorter events, 0.2 us)
Async XLA Ops:
  6.5 135.2 %copy-start = (bf16[512,2048]{1,0:T(8,128)(2,1)S(1)}, bf16[512,2048]{1,0:T(8,128)(2,1)}, u32[]{:S(2)}) copy-start(bf16[512,2048]{1,0:T(8,128)(2,1)} %param.19) | copy-start | bytes 6291460
  22.0 11.8 %copy-start.4 = (s32[64]{0:T(128)S(1)}, s32[64]{0:T(128)}, u32[]{:S(2)}) copy-start(s32[64]{0:T(128)} %param.17) | copy-start | bytes 772
  22.0 13.6 %copy-start.2 = (bf16[128,512]{1,0:T(8,128)(2,1)S(1)}, bf16[128,512]{1,0:T(8,128)(2,1)}, u32[]{:S(2)}) copy-start(bf16[128,512]{1,0:T(8,128)(2,1)} %param.12) | copy-start | bytes 393220
  22.0 63.9 %all-to-all-start = ((bf16[128,1,64,256]{3,2,1,0:T(8,128)(2,1)}), bf16[128,1,64,256]{3,2,1,0:T(8,128)(2,1)}, u32[]{:S(2)}, u32[]{:S(2)}) async-start(bf16[128,1,64,256]{3,2,1,0:T(8,128)(2,1)} %bitcast.135), calls=%async_computation | async-start | bytes 8388608 | tf_op jit(solution)/shard_map/all_to_all | solution.py:49
  33.7 108.0 %all-gather.2.cloned.1.call-start = ((), (), s32[]{:S(2)}) async-start(), calls=%async_computation.2 | async-start | bytes 1179648 | tf_op jit(solution)/shard_map/all_gather | solution.py:124
  94.3 246.4 %all-reduce.2.cloned.1.call-start = ((), (), s32[]{:S(2)}) async-start(), calls=%async_computation.3 | async-start | bytes 16777216 | tf_op jit(solution)/shard_map/psum | solution.py:130
  148.5 0.7 copy-start.3
  148.6 405.6 %reduce-scatter.2.cloned.1.call-start = ((), (), s32[]{:S(2)}) async-start(), calls=%async_computation.4 | async-start | bytes 15335424 | tf_op jit(solution)/shard_map/reduce_scatter | solution.py:135
  394.6 167.2 %copy-start.1 = (bf16[512,2048]{1,0:T(8,128)(2,1)S(1)}, bf16[512,2048]{1,0:T(8,128)(2,1)}, u32[]{:S(2)}) copy-start(bf16[512,2048]{1,0:T(8,128)(2,1)} %param.19) | copy-start | bytes 6291460
Sparse Core Ops, SparseCore 0:
  94.4 47.2 all-gather.1
  148.7 191.9 all-reduce.1
  394.7 159.4 reduce-scatter.1
where the time goes:
time: 569 us; the launch traced here: 568 us
  waiting for transfers between devices  425 us (75%)
  local copies, waits for them, and re-layouts  40.4 us (7%)
  matrix products  37.1 us (7%)
  blocking collectives  23.9 us (4%)
  other arithmetic  17.1 us (3%)
  between operations  13.3 us (2%)
  starting transfers between devices  11.8 us (2%)
    psum x1, waiting for transfers between devices, per_device(): carried = residual.astype(jnp.float32) + lax.psum(partial_out, 'tensor')  177 us
    reduce_scatter x1, waiting for transfers between devices, per_device(): lax.psum_scatter(jnp.dot(normed, weights_local, preferred_element_type=jn...  160 us
    all_gather x1, waiting for transfers between devices, per_device(): lax.all_gather(attended, 'replica', axis=0, tiled=True)  47.4 us
    all_to_all x1, waiting for transfers between devices, per_device(): lax.all_to_all(outgoing, ('replica', 'tensor'), split_axis=0, concat_axis...  40.4 us
    dot_general x1, matrix products, per_device(): jnp.dot(normed, weights_local, preferred_element_type=jnp.float32)  24.2 us
    psum x1, blocking collectives, per_device(): squares = lax.psum(jnp.sum(carried * carried, axis=1), 'replica')  23.9 us
    unnamed x13, local copies, waits for them, and re-layouts  15 us
    all_to_all x1, starting transfers between devices, per_device(): lax.all_to_all(outgoing, ('replica', 'tensor'), split_axis=0, concat_axis...  11.7 us
  transfers between devices with their start and end apart: 4, of which 4 were waited for; matrix products, arithmetic and copies ran while one was open for 5% of the time, Pallas kernels for 0%

commit v1 on v0

--- a/solution.py
+++ b/solution.py
@@ -121,7 +121,10 @@
     back_index = row_slot * slot_rows + row_ids - jnp.take(starts, row_slot, axis=0)
     attended = jnp.take(slot_attended, back_index, axis=0)
     partial_out = jnp.dot(
-        lax.all_gather(attended, "replica", axis=0, tiled=True),
+        jnp.concatenate(
+            lax.all_to_all(jnp.stack([attended] * lax.axis_size("replica")), "replica", 0, 0),
+            axis=0,
+        ),
         out_weight,
         preferred_element_type=jnp.float32,
     )

time: 569 us -> 540 us (0.949)
  waiting for transfers between devices: 425 us -> 378 us
  blocking collectives: 23.9 us -> 43.4 us
    all_gather x1 -> x0, waiting for transfers between devices: 47.4 us -> none  [per_device(): lax.all_gather(attended, 'replica', axis=0, tiled=True)]
    all_to_all x0 -> x1, blocking collectives: none -> 19.8 us  [per_device(): lax.all_to_all(jnp.stack([attended] * lax.axis_size('replica')), 'replica...]
  transfers between devices with their start and end apart: 4 -> 3, of which waited for: 4 -> 3; matrix products, arithmetic and copies ran while one was open for 5% -> 5% of each run, Pallas kernels for 0% -> 0%
where the time goes in v1:
time: 540 us; the launch traced here: 539 us
  waiting for transfers between devices  378 us (70%)
  blocking collectives  43.4 us (8%)
  local copies, waits for them, and re-layouts  40.3 us (7%)
  matrix products  35.9 us (7%)
  other arithmetic  16.5 us (3%)
  between operations  13.7 us (3%)
  starting transfers between devices  12 us (2%)
    psum x1, waiting for transfers between devices, per_device(): carried = residual.astype(jnp.float32) + lax.psum(partial_out, 'tensor')  178 us
    reduce_scatter x1, waiting for transfers between devices, per_device(): lax.psum_scatter(jnp.dot(normed, weights_local, preferred_element_type=jn...  160 us
    all_to_all x1, waiting for transfers between devices, per_device(): lax.all_to_all(outgoing, ('replica', 'tensor'), split_axis=0, concat_axis...  40.4 us
    dot_general x1, matrix products, per_device(): jnp.dot(normed, weights_local, preferred_element_type=jnp.float32)  24.2 us
    psum x1, blocking collectives, per_device(): squares = lax.psum(jnp.sum(carried * carried, axis=1), 'replica')  23.7 us
    all_to_all x1, blocking collectives, per_device(): lax.all_to_all(jnp.stack([attended] * lax.axis_size('replica')), 'replica...  19.8 us
    unnamed x13, local copies, waits for them, and re-layouts  14.8 us
    all_to_all x1, starting transfers between devices, per_device(): lax.all_to_all(outgoing, ('replica', 'tensor'), split_axis=0, concat_axis...  11.7 us
  transfers between devices with their start and end apart: 3, of which 3 were waited for; matrix products, arithmetic and copies ran while one was open for 5% of the time, Pallas kernels for 0%

profile of v1, /device:TPU:0, one launch (start us, length us, event | category | flops | bytes accessed | tf_op | source)
XLA Modules:
  0.0 539.2 jit_solution(1322887215405611842)
XLA Ops:
  6.5 0.0 copy-start
  6.5 0.9 constant_dynamic-slice_fusion
  7.4 0.1 copy.62
  7.6 0.8 dynamic-slice_bitcast_fusion
  8.3 0.6 gather_fusion
  9.0 0.7 pad_clamp_fusion.2
  9.7 1.8 gather_fusion.1
  11.5 1.6 gather.42
  13.1 1.4 fusion.18
  14.5 2.8 gather_fusion.2
  17.3 4.7 copy.48
  22.0 0.0 copy-start.4
  22.0 0.0 copy-start.2
  22.0 11.7 %all-to-all-start = ((bf16[128,1,64,256]{3,2,1,0:T(8,128)(2,1)}), bf16[128,1,64,256]{3,2,1,0:T(8,128)(2,1)}, u32[]{:S(2)}, u32[]{:S(2)}) async-start(bf16[128,1,64,256]{3,2,1,0:T(8,128)(2,1)} %bitcast.136), calls=%async_computation | async-start | bytes 8388608 | tf_op jit(solution)/shard_map/all_to_all | solution.py:49
  33.7 0.0 all-reduce.2.cloned.1.call-start
  33.8 0.0 copy-done.4
  33.8 0.1 dynamic_slice.19
  33.9 0.7 fusion.33
  34.5 0.2 reduce-window.7
  34.7 0.7 bitcast_subtract_fusion.1
  35.4 0.1 add_minimum_fusion
  35.5 0.1 min.22
  35.6 0.0 copy-done.2
  35.7 0.9 constant_dynamic-slice_fusion.1
  36.5 1.1 gather_fusion.4
  37.7 1.0 gather_fusion.3
  38.7 0.7 fusion.39
  39.4 0.1 convert_reduce_fusion
  39.5 4.9 compare_and_fusion.1
  44.4 0.1 compare_and_fusion
  44.4 0.1 iota_compare_fusion.2
  44.5 0.1 iota_compare_fusion
  44.6 0.1 broadcast_and_fusion
  44.7 0.1 broadcast_select_fusion.2
  44.8 0.6 fusion.40
  45.4 40.4 %all-to-all-done = bf16[128,1,64,256]{3,2,1,0:T(8,128)(2,1)} async-done(((bf16[128,1,64,256]{3,2,1,0:T(8,128)(2,1)}), bf16[128,1,64,256]{3,2,1,0:T(8,128)(2,1)}, u32[]{:S(2)}, u32[]{:S(2)}) %all-to-all-start) | async-done | bytes 4194336 | tf_op jit(solution)/shard_map/all_to_all | solution.py:49
  85.8 2.4 bitcast_reduce_fusion
  88.3 2.7 fusion.6
  91.0 1.0 fusion.4
  92.0 0.1 fusion.21
  92.2 0.3 fusion.17
  92.5 0.1 copy.54
  92.7 0.8 gather_fusion.5
  93.5 0.1 broadcast_select_fusion.1
  93.6 0.1 stack.2
  93.7 19.8 %all_to_all.10 = bf16[8,128,512]{2,1,0:T(8,128)(2,1)S(1)} all-to-all(bf16[8,128,512]{2,1,0:T(8,128)(2,1)S(1)} %stack.2), channel_id=1, replica_groups=mesh['replica'=8,'tensor'=16] {'replica'}, dimensions={0} | all-to-all | bytes 2097152 | tf_op jit(solution)/shard_map/all_to_all | solution.py:125
  113.5 0.0 copy-done
  113.5 5.6 %fusion.41 = f32[1024,2048]{1,0:T(8,128)} fusion(bf16[1024,512]{1,0:T(8,128)(2,1)S(1)} %bitcast.141, bf16[512,2048]{1,0:T(8,128)(2,1)S(1)} %copy-done), kind=kOutput, calls=%fused_computation.105 | convolution fusion | flops 2147483648 | bytes 11534336 | tf_op jit(solution)/shard_map/dot_general | solution.py:123
  119.1 0.0 copy-start.3
  119.1 0.0 all-reduce.2.cloned.1.call-update
  119.1 0.2 reduce-scatter.2.cloned.1.call-start
  119.3 0.4 copy-done.3
  119.8 14.3 %copy.66 = bf16[256,8,2,1664]{3,1,2,0:T(8,128)(2,1)} copy(bf16[256,8,2,1664]{3,2,1,0:T(2,128)(2,1)} %bitcast.138) | data formatting | bytes 27262976
  134.0 177.5 %all-reduce.2.cloned.1.call-done = f32[1024,2048]{1,0:T(8,128)} async-done(((f32[1024,2048]{1,0:T(8,128)}), f32[1024,2048]{1,0:T(8,128)}) %all-reduce.2.cloned.1.call-update) | async-done | bytes 8388624 | tf_op jit(solution)/shard_map/psum | solution.py:133
  311.6 5.7 %multiply_reduce_fusion = f32[1024]{0:T(1024)S(1)} fusion(f32[1024,2048]{1,0:T(8,128)} %all-reduce.2.cloned.1.call-done, bf16[1024,2048]{1,0:T(8,128)(2,1)} %param.20), kind=kLoop, calls=%fused_computation.7 | loop fusion | flops 8387584 | bytes 12587008 | tf_op jit(solution)/shard_map/reduce_sum | solution.py:134
  317.3 23.7 %psum.15 = f32[1024]{0:T(1024)S(1)} all-reduce(f32[1024]{0:T(1024)S(1)} %multiply_reduce_fusion), channel_id=1, replica_groups=mesh['replica'=8,'tensor'=16] {'replica'}, use_global_device_ids=true, to_apply=%region_8.9 | all-reduce | flops 1024 | bytes 8192 | tf_op jit(solution)/shard_map/psum | solution.py:134
  341.0 24.2 %fusion = f32[1024,3328]{1,0:T(8,128)} fusion(bf16[2048,3328]{1,0:T(8,128)(2,1)} %bitcast.139, f32[1024,2048]{1,0:T(8,128)} %all-reduce.2.cloned.1.call-done, bf16[1024,2048]{1,0:T(8,128)(2,1)} %param.20, f32[2048]{0:T(1024)S(1)} %convert_element_type.29, f32[1024]{0:T(1024)S(1)} %add_rsqrt_fusion), kind=kOutput, calls=%fused_computation.9 | convolution fusion | flops 13969129472 | bytes 39858176 | tf_op jit(solution)/shard_map/dot_general | solution.py:139
  365.2 0.0 reduce-scatter.2.cloned.1.call-update
  365.2 0.0 copy-start.1
  365.3 159.6 %reduce-scatter.2.cloned.1.call-done = f32[128,3328]{1,0:T(8,128)} async-done(((f32[1024,3328]{1,0:T(8,128)}), f32[128,3328]{1,0:T(8,128)}) %reduce-scatter.2.cloned.1.call-update) | async-done | bytes 1703952 | tf_op jit(solution)/shard_map/reduce_scatter | solution.py:138
  524.8 3.1 reshape.278
  528.0 3.4 fusion.38
  531.4 1.0 fusion.20
  532.4 0.0 copy-done.1
  (16 shorter events, 0.2 us)
Async XLA Ops:
  6.5 106.9 %copy-start = (bf16[512,2048]{1,0:T(8,128)(2,1)S(1)}, bf16[512,2048]{1,0:T(8,128)(2,1)}, u32[]{:S(2)}) copy-start(bf16[512,2048]{1,0:T(8,128)(2,1)} %param.19) | copy-start | bytes 6291460
  22.0 11.8 %copy-start.4 = (s32[64]{0:T(128)S(1)}, s32[64]{0:T(128)}, u32[]{:S(2)}) copy-start(s32[64]{0:T(128)} %param.17) | copy-start | bytes 772
  22.0 13.6 %copy-start.2 = (bf16[128,512]{1,0:T(8,128)(2,1)S(1)}, bf16[128,512]{1,0:T(8,128)(2,1)}, u32[]{:S(2)}) copy-start(bf16[128,512]{1,0:T(8,128)(2,1)} %param.12) | copy-start | bytes 393220
  22.0 63.9 %all-to-all-start = ((bf16[128,1,64,256]{3,2,1,0:T(8,128)(2,1)}), bf16[128,1,64,256]{3,2,1,0:T(8,128)(2,1)}, u32[]{:S(2)}, u32[]{:S(2)}) async-start(bf16[128,1,64,256]{3,2,1,0:T(8,128)(2,1)} %bitcast.136), calls=%async_computation | async-start | bytes 8388608 | tf_op jit(solution)/shard_map/all_to_all | solution.py:49
  33.7 277.9 %all-reduce.2.cloned.1.call-start = ((), (), s32[]{:S(2)}) async-start(), calls=%async_computation.3 | async-start | bytes 16777216 | tf_op jit(solution)/shard_map/psum | solution.py:133
  119.1 0.7 copy-start.3
  119.1 405.7 %reduce-scatter.2.cloned.1.call-start = ((), (), s32[]{:S(2)}) async-start(), calls=%async_computation.4 | async-start | bytes 15335424 | tf_op jit(solution)/shard_map/reduce_scatter | solution.py:138
  365.2 167.2 %copy-start.1 = (bf16[512,2048]{1,0:T(8,128)(2,1)S(1)}, bf16[512,2048]{1,0:T(8,128)(2,1)}, u32[]{:S(2)}) copy-start(bf16[512,2048]{1,0:T(8,128)(2,1)} %param.19) | copy-start | bytes 6291460
Sparse Core Ops, SparseCore 0:
  119.2 192.2 all-reduce.1
  365.4 159.4 reduce-scatter.1
